TPU v7x, 128 devices: a whole 4x4x4 slice. The times are simulated.
128 devices in a mesh: section: 2 (over x_hi), dp: 8 (over z, core), mp: 8 (over x_lo, y).
Axes of the slice: x: 4 (x_hi: 2, x_lo: 2; x = x_hi * 2 + x_lo), y: 4, z: 4, core: 2. Of those that a mesh axis runs over, the one named last changes fastest.
Arguments:
- inputs: bfloat16 [2, 16, 128, 4096], P('section', 'dp'), may hold values from -6 to 6
- norm_gains: bfloat16 [2, 4096], P('section'), may hold values from 0.5 to 1.5
- weights: bfloat16 [2, 4096, 4, 4096], P('section', 'dp', None, 'mp'), may hold values from -0.09375 to 0.09375
- cotangent: bfloat16 [16, 128, 4096], P('dp'), may hold values from -6 to 6
- lengths: int32 [2, 16], P(None, 'dp'), may hold values from 32 to 128, as said below
- dp_noise: float32 [2, 4096, 4, 4096], P('section', 'dp', None, 'mp'), may hold values from -6 to 6
Outputs:
- noisy_grad: float32 [2, 4096, 4, 4096], P('section', 'dp', None, 'mp')
- clip_scale: float32 [16], P('dp')
Inputs may be any that keep to these rules, and one draw needn't show every extreme that they name: `lengths`: the first example of each row has length 128.
All inputs are finite; a program needn't handle non-finite values.
Results may differ from a plain program's by a relative error of at most 0.024.
Values may be sent and summed in bfloat16 or wider, within the bound.
A program may use at most 256 MiB of HBM per device.

v0:
```python
import jax
import jax.numpy as jnp
from jax import lax
from jax.sharding import PartitionSpec as P

D = 4096
HEADS = 64
HEAD = 64


def from_partner(x, axis, distance):
    return lax.ppermute(x, axis, [(i, i ^ 1 << distance) for i in range(lax.axis_size(axis))])


def rms_norm(values_in, gain_row):
    value32 = values_in.astype(jnp.float32)
    inverse = lax.rsqrt(jnp.mean(value32 * value32, axis=-1, keepdims=True) + 1e-06)
    return (value32 * inverse * gain_row.astype(jnp.float32)).astype(jnp.bfloat16)


def project(left, right):
    return jnp.dot(left, right, preferred_element_type=jnp.float32).astype(jnp.bfloat16)


def attend(queries, key_proj, value_proj, key_mask):
    seq_len = queries.shape[0]
    query_heads = queries.reshape(seq_len, -1, HEAD)
    key_heads = key_proj.reshape(seq_len, -1, HEAD)
    value_heads = value_proj.reshape(seq_len, -1, HEAD)
    scores = jnp.einsum(
        "shd,thd->hst", query_heads, key_heads, preferred_element_type=jnp.float32
    ) * HEAD ** (-0.5)
    scores = jnp.where(key_mask[None, None, :], scores, -jnp.inf)
    attn_probs = jax.nn.softmax(scores, axis=-1)
    probs_low = attn_probs.astype(jnp.bfloat16)
    context = jnp.einsum("hst,thd->shd", probs_low, value_heads, preferred_element_type=jnp.float32)
    return (attn_probs, context.reshape(seq_len, -1).astype(jnp.bfloat16))


def attend_back(queries, key_proj, value_proj, attn_probs, grad_ctx):
    seq_len = queries.shape[0]
    query_heads = queries.reshape(seq_len, -1, HEAD)
    key_heads = key_proj.reshape(seq_len, -1, HEAD)
    value_heads = value_proj.reshape(seq_len, -1, HEAD)
    grad_heads = grad_ctx.reshape(seq_len, -1, HEAD)
    grad_probs = jnp.einsum(
        "shd,thd->hst", grad_heads, value_heads, preferred_element_type=jnp.float32
    )
    inner_sum = jnp.sum(grad_probs * attn_probs, axis=-1, keepdims=True)
    grad_scores = (attn_probs * (grad_probs - inner_sum) * HEAD ** (-0.5)).astype(jnp.bfloat16)
    probs_low = attn_probs.astype(jnp.bfloat16)
    grad_query = jnp.einsum(
        "hst,thd->shd", grad_scores, key_heads, preferred_element_type=jnp.float32
    )
    grad_key = jnp.einsum(
        "hst,shd->thd", grad_scores, query_heads, preferred_element_type=jnp.float32
    )
    grad_value = jnp.einsum(
        "hst,shd->thd", probs_low, grad_heads, preferred_element_type=jnp.float32
    )
    return (
        grad_query.reshape(seq_len, -1).astype(jnp.bfloat16),
        grad_key.reshape(seq_len, -1).astype(jnp.bfloat16),
        grad_value.reshape(seq_len, -1).astype(jnp.bfloat16),
    )


def gram(matrix):
    return jnp.dot(matrix, matrix.T, preferred_element_type=jnp.float32)


def ghost(normed, kv_rows, grad_query, grad_key, grad_value, grad_out, context):
    first = jnp.sum(gram(normed) * gram(grad_query))
    second = jnp.sum(gram(kv_rows) * (gram(grad_key) + gram(grad_value)))
    third = jnp.sum(gram(grad_out) * gram(context))
    return first + second + third


def get_row(buffer, index):
    return lax.dynamic_index_in_dim(buffer, index, 0, keepdims=False)


def put_row(buffer, value, index, valid):
    current = get_row(buffer, index)
    return lax.dynamic_update_index_in_dim(buffer, jnp.where(valid, value, current), index, 0)


def per_device(inputs, norm_gains, weights, cotangent, lengths, dp_noise):
    section_index = lax.axis_index("section")
    is_dec = section_index == 1
    micro_count = inputs.shape[1]
    seq_len = inputs.shape[2]
    width = inputs.shape[3]
    gathered = lax.all_gather(weights, "dp", axis=1, tiled=True)[0]
    inner_dev = gathered.shape[2]
    own_inputs = inputs[0]
    gain_row = norm_gains[0]
    positions = jnp.arange(seq_len)
    wide_zero = jnp.zeros((micro_count, seq_len, width), jnp.bfloat16)
    thin_zero = jnp.zeros((micro_count, seq_len, inner_dev), jnp.bfloat16)
    normed_buf, kv_buf, gout_buf = (wide_zero, wide_zero, wide_zero)
    query_buf, key_buf, value_buf, context_buf = (thin_zero, thin_zero, thin_zero, thin_zero)
    gq_buf, gk_buf, gv_buf = (thin_zero, thin_zero, thin_zero)
    probs_buf = jnp.zeros((micro_count, inner_dev // HEAD, seq_len, seq_len), jnp.float32)
    norm_parts = jnp.zeros((micro_count,), jnp.float32)
    incoming = jnp.zeros((seq_len, width), jnp.bfloat16)
    for step_num in range(micro_count + 2):
        fwd_mb = step_num - section_index
        fwd_ok = (fwd_mb >= 0) & (fwd_mb < micro_count)
        fwd_idx = jnp.clip(fwd_mb, 0, micro_count - 1)
        rows_now = get_row(own_inputs, fwd_idx)
        normed = rms_norm(rows_now, gain_row)
        kv_rows = jnp.where(is_dec, incoming, normed)
        queries = project(normed, gathered[:, 0])
        key_proj = project(kv_rows, gathered[:, 1])
        value_proj = project(kv_rows, gathered[:, 2])
        key_mask = positions < get_row(lengths[0], fwd_idx)
        attn_probs, context_new = attend(queries, key_proj, value_proj, key_mask)
        normed_buf = put_row(normed_buf, normed, fwd_idx, fwd_ok)
        kv_buf = put_row(kv_buf, kv_rows, fwd_idx, fwd_ok)
        query_buf = put_row(query_buf, queries, fwd_idx, fwd_ok)
        key_buf = put_row(key_buf, key_proj, fwd_idx, fwd_ok)
        value_buf = put_row(value_buf, value_proj, fwd_idx, fwd_ok)
        probs_buf = put_row(probs_buf, attn_probs, fwd_idx, fwd_ok)
        context_buf = put_row(context_buf, context_new, fwd_idx, fwd_ok)
        bwd_mb = step_num - 2 + section_index
        bwd_ok = (bwd_mb >= 0) & (bwd_mb < micro_count)
        bwd_idx = jnp.clip(bwd_mb, 0, micro_count - 1)
        dec_mask = (positions < get_row(lengths[1], bwd_idx)).astype(jnp.bfloat16)
        cot_rows = get_row(cotangent, bwd_idx) * dec_mask[:, None]
        grad_out = jnp.where(is_dec, cot_rows, incoming)
        grad_ctx = project(grad_out, gathered[:, 3])
        back_query = get_row(query_buf, bwd_idx)
        back_key = get_row(key_buf, bwd_idx)
        back_value = get_row(value_buf, bwd_idx)
        back_context = get_row(context_buf, bwd_idx)
        grad_query, grad_key, grad_value = attend_back(
            back_query, back_key, back_value, get_row(probs_buf, bwd_idx), grad_ctx
        )
        sq_part = ghost(
            get_row(normed_buf, bwd_idx),
            get_row(kv_buf, bwd_idx),
            grad_query,
            grad_key,
            grad_value,
            grad_out,
            back_context,
        )
        gout_buf = put_row(gout_buf, grad_out, bwd_idx, bwd_ok)
        gq_buf = put_row(gq_buf, grad_query, bwd_idx, bwd_ok)
        gk_buf = put_row(gk_buf, grad_key, bwd_idx, bwd_ok)
        gv_buf = put_row(gv_buf, grad_value, bwd_idx, bwd_ok)
        slot_hit = bwd_ok & (jnp.arange(micro_count) == bwd_idx)
        norm_parts = jnp.where(slot_hit, sq_part, norm_parts)
        if step_num < micro_count + 1:
            relay_term = lax.cond(
                is_dec,
                lambda: jnp.einsum(
                    "sj,dj->sd", grad_key, gathered[:, 1], preferred_element_type=jnp.float32
                )
                + jnp.einsum(
                    "sj,dj->sd", grad_value, gathered[:, 2], preferred_element_type=jnp.float32
                ),
                lambda: jnp.einsum(
                    "sj,dj->sd", context_new, gathered[:, 3], preferred_element_type=jnp.float32
                ),
            )
            residual = jnp.where(is_dec, 0.0, rows_now.astype(jnp.float32))
            summed_rows = lax.psum(relay_term.astype(jnp.bfloat16), "mp").astype(jnp.float32)
            payload = (summed_rows + residual).astype(jnp.bfloat16)
            incoming = from_partner(payload, "section", 0)
    sq_norm = lax.psum(norm_parts, ("section", "mp"))
    bound = jnp.sqrt(jnp.float32(8.0 * D * HEADS * HEAD))
    clip_scale = bound / (jnp.sqrt(sq_norm) + 0.01 * bound)
    totals = jnp.zeros((weights.shape[1] * lax.axis_size("dp"), 4, inner_dev), jnp.float32)
    for micro_num in range(micro_count):
        normed_cols = normed_buf[micro_num]
        kv_cols = kv_buf[micro_num]
        gout_cols = gout_buf[micro_num]
        stacked = jnp.stack(
            [
                jnp.einsum(
                    "sd,sj->dj", normed_cols, gq_buf[micro_num], preferred_element_type=jnp.float32
                ),
                jnp.einsum(
                    "sd,sj->dj", kv_cols, gk_buf[micro_num], preferred_element_type=jnp.float32
                ),
                jnp.einsum(
                    "sd,sj->dj", kv_cols, gv_buf[micro_num], preferred_element_type=jnp.float32
                ),
                jnp.einsum(
                    "sd,sj->dj",
                    gout_cols,
                    context_buf[micro_num],
                    preferred_element_type=jnp.float32,
                ),
            ],
            axis=1,
        )
        totals = totals + clip_scale[micro_num] * stacked
    summed = lax.psum_scatter(
        totals.astype(jnp.bfloat16), "dp", scatter_dimension=0, tiled=True
    ).astype(jnp.float32)
    examples_total = micro_count * lax.axis_size("dp")
    noisy_grad = (summed + dp_noise[0]) / examples_total
    return (noisy_grad[None], clip_scale)


def solution(mesh):
    placed = (
        P("section", "dp", None, None),
        P("section", None),
        P("section", "dp", None, "mp"),
        P("dp", None, None),
        P(None, "dp"),
        P("section", "dp", None, "mp"),
    )
    return jax.shard_map(
        per_device,
        mesh=mesh,
        in_specs=placed,
        out_specs=(P("section", "dp", None, "mp"), P("dp")),
        check_vma=False,
    )
```

profile of v0, /device:TPU:1, one launch (start us, length us, event | category | flops | bytes accessed | tf_op | source)
XLA Modules:
  0.0 845.7 jit_solution(15828079697014097432)
XLA Ops:
  38.8 60.7 %all-gather.2.cloned.1.call-done = bf16[1,4096,4,512]{3,1,2,0:T(8,128)(2,1)} async-done(((bf16[1,512,4,512]{3,1,2,0:T(8,128)(2,1)}), bf16[1,4096,4,512]{3,1,2,0:T(8,128)(2,1)}) %all-gather.2.cloned.1.call-update) | async-done | bytes 16777232 | tf_op jit(solution)/shard_map/all_gather | solution.py:94
  130.8 4.8 conditional.3
  130.8 4.8 fusion
  148.2 63.0 %all-reduce.4.cloned.1.call-done = bf16[128,4096]{1,0:T(8,128)(2,1)} async-done(((bf16[128,4096]{1,0:T(8,128)(2,1)}), bf16[128,4096]{1,0:T(8,128)(2,1)}) %all-reduce.4.cloned.1.call-update) | async-done | bytes 1048592 | tf_op jit(solution)/shard_map/psum | solution.py:169
  245.4 6.0 bitcast_dynamic-update-slice_fusion.5
  299.0 4.9 conditional.4
  315.2 70.6 %all-reduce.6.cloned.1.call-done = bf16[128,4096]{1,0:T(8,128)(2,1)} async-done(((bf16[128,4096]{1,0:T(8,128)(2,1)}), bf16[128,4096]{1,0:T(8,128)(2,1)}) %all-reduce.6.cloned.1.call-update) | async-done | bytes 1048592 | tf_op jit(solution)/shard_map/psum | solution.py:169
  395.2 12.4 %collective-permute-done.1 = bf16[128,4096]{1,0:T(8,128)(2,1)S(1)} collective-permute-done((bf16[128,4096]{1,0:T(8,128)(2,1)S(1)}, bf16[128,4096]{1,0:T(8,128)(2,1)S(1)}, u32[]{:S(2)}, u32[]{:S(2)}) %collective-permute-start.1) | collective-permute-done | bytes 1048608 | tf_op jit(solution)/shard_map/ppermute | solution.py:12
  407.6 4.8 bitcast_dynamic-update-slice_fusion.4
  460.9 4.8 conditional.5
  476.4 72.0 %all-reduce.8.cloned.1.call-done = bf16[128,4096]{1,0:T(8,128)(2,1)} async-done(((bf16[128,4096]{1,0:T(8,128)(2,1)}), bf16[128,4096]{1,0:T(8,128)(2,1)}) %all-reduce.8.cloned.1.call-update) | async-done | bytes 1048592 | tf_op jit(solution)/shard_map/psum | solution.py:169
  558.3 12.4 %collective-permute-done.2 = bf16[128,4096]{1,0:T(8,128)(2,1)S(1)} collective-permute-done((bf16[128,4096]{1,0:T(8,128)(2,1)S(1)}, bf16[128,4096]{1,0:T(8,128)(2,1)S(1)}, u32[]{:S(2)}, u32[]{:S(2)}) %collective-permute-start.2) | collective-permute-done | bytes 1048608 | tf_op jit(solution)/shard_map/ppermute | solution.py:12
  570.7 4.8 bitcast_dynamic-update-slice_fusion.3
  604.4 5.7 convolution_bitcast_fusion.1
  610.1 5.7 convolution_bitcast_fusion.5
  615.8 5.7 convolution_bitcast_fusion.2
  621.5 5.7 convolution_bitcast_fusion.6
  629.2 5.9 convolution_bitcast_fusion
  635.1 5.7 convolution_bitcast_fusion.4
  654.0 5.7 convolution_bitcast_fusion.3
  662.1 5.8 convolution_bitcast_fusion.7
  667.9 31.8 %psum.31 = f32[2]{0:T(128)S(1)} all-reduce(f32[2]{0:T(128)S(1)} %and_select_fusion.3), channel_id=1, replica_groups=mesh['section'=2,'dp'=8,'mp'=8] {'section','mp'}, use_global_device_ids=true, to_apply=%region_37.38 | all-reduce | flops 2 | bytes 16 | tf_op jit(solution)/shard_map/psum | solution.py:172
  700.3 28.8 %fusion.33 = bf16[4096,4,512]{2,0,1:T(8,128)(2,1)} fusion(f32[4096,1,512]{2,0,1:T(8,128)} %convolution_bitcast_fusion.4, f32[4096,1,512]{2,0,1:T(8,128)} %convolution_bitcast_fusion.5, f32[4096,1,512]{2,0,1:T(8,128)} %convolution_bitcast_fusion.6, f32[4096,1,512]{2,0,1:T(8,128)} %convolution_bitcast_fusion.7, f32[4096,1,512]{2,0,1:T(8,128)} %convolution_bitcast_fusion, ...), kind=kLoop, calls=%fused_computation.37 | loop fusion | flops 83886080 | bytes 83886088 | tf_op jit(solution)/shard_map/convert_element_type | solution.py:202
  729.1 100.7 %reduce-scatter.2.cloned.1.call-done = bf16[512,4,512]{2,0,1:T(8,128)(2,1)} async-done(((bf16[4096,4,512]{2,0,1:T(8,128)(2,1)}), bf16[512,4,512]{2,0,1:T(8,128)(2,1)}) %reduce-scatter.2.cloned.1.call-update) | async-done | bytes 2097168 | tf_op jit(solution)/shard_map/reduce_scatter | solution.py:201
  (314 shorter events, 304.8 us)
Async XLA Ops:
  7.2 92.3 %all-gather.2.cloned.1.call-start = ((), (), s32[]{:S(2)}) async-start(), calls=%async_computation.1 | async-start | bytes 18874368 | tf_op jit(solution)/shard_map/all_gather | solution.py:94
  10.6 200.7 %all-reduce.4.cloned.1.call-start = ((), (), s32[]{:S(2)}) async-start(), calls=%async_computation.2 | async-start | bytes 2097152 | tf_op jit(solution)/shard_map/psum | solution.py:169
  21.3 86.0 %copy-start.38 = (f32[128]{0:T(128)}, f32[128]{0:T(128)S(1)}, u32[]{:S(2)}) copy-start(f32[128]{0:T(128)S(1)} %add_rsqrt_fusion.3) | copy-start | bytes 1540
  135.6 250.2 %all-reduce.6.cloned.1.call-start = ((), (), s32[]{:S(2)}) async-start(), calls=%async_computation.3 | async-start | bytes 2097152 | tf_op jit(solution)/shard_map/psum | solution.py:169
  224.9 20.6 %collective-permute-start = (bf16[128,4096]{1,0:T(8,128)(2,1)}, bf16[128,4096]{1,0:T(8,128)(2,1)}, u32[]{:S(2)}, u32[]{:S(2)}) collective-permute-start(bf16[128,4096]{1,0:T(8,128)(2,1)} %get-tuple-element.111), channel_id=1, source_target_pairs={{0,64},{64,0},{1,65},{65,1},{2,66},{66,2},{3,67},{67,3},{4,68},{68... | collective-permute-start | bytes 3145736 | tf_op jit(solution)/shard_map/ppermute | solution.py:12
  303.9 244.5 %all-reduce.8.cloned.1.call-start = ((), (), s32[]{:S(2)}) async-start(), calls=%async_computation.4 | async-start | bytes 2097152 | tf_op jit(solution)/shard_map/psum | solution.py:169
  304.7 7.4 copy-start.22
  306.3 7.3 copy-start.21
  387.3 20.3 %collective-permute-start.1 = (bf16[128,4096]{1,0:T(8,128)(2,1)S(1)}, bf16[128,4096]{1,0:T(8,128)(2,1)S(1)}, u32[]{:S(2)}, u32[]{:S(2)}) collective-permute-start(bf16[128,4096]{1,0:T(8,128)(2,1)S(1)} %fusion.67), channel_id=1, source_target_pairs={{0,64},{64,0},{1,65},{65,1},{2,66},{66,2},{3,67},{67,3},{4,68},{68... | collective-permute-start | bytes 3145736 | tf_op jit(solution)/shard_map/ppermute | solution.py:12
  392.4 15.2 %copy-start.4 = (bf16[2,128,4096]{2,1,0:T(8,128)(2,1)S(1)}, bf16[2,128,4096]{2,1,0:T(8,128)(2,1)}, u32[]{:S(2)}) copy-start(bf16[2,128,4096]{2,1,0:T(8,128)(2,1)} %param.15) | copy-start | bytes 6291460
  392.4 15.2 %copy-start.42 = (f32[128]{0:T(128)S(1)}, f32[128]{0:T(128)}, u32[]{:S(2)}) copy-start(f32[128]{0:T(128)} %add_rsqrt_fusion.1) | copy-start | bytes 1540
  392.4 15.2 %copy-start.46 = (bf16[128]{0:T(256)(128)(2,1)S(1)}, bf16[128]{0:T(256)(128)(2,1)}, u32[]{:S(2)}) copy-start(bf16[128]{0:T(256)(128)(2,1)} %compare_convert_fusion.1) | copy-start | bytes 772
  465.7 364.2 %reduce-scatter.2.cloned.1.call-start = ((), (), s32[]{:S(2)}) async-start(), calls=%async_computation.5 | async-start | bytes 18874368 | tf_op jit(solution)/shard_map/reduce_scatter | solution.py:201
  466.3 7.0 copy-start.24
  466.3 8.5 %copy-start.23 = (bf16[1,128,512]{2,1,0:T(8,128)(2,1)S(1)}, bf16[1,128,512]{2,1,0:T(8,128)(2,1)}, u32[]{:S(2)}) copy-start(bf16[1,128,512]{2,1,0:T(8,128)(2,1)} %copy.138) | copy-start | bytes 393220
  550.0 20.7 %collective-permute-start.2 = (bf16[128,4096]{1,0:T(8,128)(2,1)S(1)}, bf16[128,4096]{1,0:T(8,128)(2,1)S(1)}, u32[]{:S(2)}, u32[]{:S(2)}) collective-permute-start(bf16[128,4096]{1,0:T(8,128)(2,1)S(1)} %fusion.77), channel_id=1, source_target_pairs={{0,64},{64,0},{1,65},{65,1},{2,66},{66,2},{3,67},{67,3},{4,68},{68... | collective-permute-start | bytes 3145736 | tf_op jit(solution)/shard_map/ppermute | solution.py:12
  555.5 15.2 %copy-start.5 = (bf16[2,128,4096]{2,1,0:T(8,128)(2,1)S(1)}, bf16[2,128,4096]{2,1,0:T(8,128)(2,1)}, u32[]{:S(2)}) copy-start(bf16[2,128,4096]{2,1,0:T(8,128)(2,1)} %param.15) | copy-start | bytes 6291460
  555.5 15.2 %copy-start.41 = (f32[128]{0:T(128)S(1)}, f32[128]{0:T(128)}, u32[]{:S(2)}) copy-start(f32[128]{0:T(128)} %add_rsqrt_fusion) | copy-start | bytes 1540
  555.5 15.2 %copy-start.45 = (bf16[128]{0:T(256)(128)(2,1)S(1)}, bf16[128]{0:T(256)(128)(2,1)}, u32[]{:S(2)}) copy-start(bf16[128]{0:T(256)(128)(2,1)} %compare_convert_fusion) | copy-start | bytes 772
  579.5 6.4 copy-start.30
  585.9 7.0 copy-start.9
  589.5 9.8 %copy-start.11 = (f32[1,8,128,128]{2,3,1,0:T(8,128)S(1)}, f32[1,8,128,128]{2,3,1,0:T(8,128)}, u32[]{:S(2)}) copy-start(f32[1,8,128,128]{2,3,1,0:T(8,128)} %constant_dynamic-slice_fusion.13) | copy-start | bytes 1572868
  635.1 9.2 %copy-start.20 = (bf16[8,64,128]{2,1,0:T(8,128)(2,1)S(1)}, bf16[8,64,128]{2,1,0:T(8,128)(2,1)}, u32[]{:S(2)}) copy-start(bf16[8,64,128]{2,1,0:T(8,128)(2,1)} %copy-done.19) | copy-start | bytes 393220
  699.7 29.4 %copy-start.40 = (f32[2]{0:T(128)}, f32[2]{0:T(128)S(1)}, u32[]{:S(2)}) copy-start(f32[2]{0:T(128)S(1)} %add_divide_fusion) | copy-start | bytes 28
  (33 other events, 119.0 us)
Sparse Core Ops, SparseCore 0:
  10.7 88.7 all-gather.1
  135.7 75.4 all-reduce.3
  304.0 81.6 all-reduce.5
  465.8 82.5 all-reduce.7
  729.2 100.5 reduce-scatter.1
where the time goes:
time: 857 us; the launch traced here: 846 us
  waiting for transfers between devices  395 us (46%)
  matrix products  202 us (24%)
  other arithmetic  95.5 us (11%)
  local copies, waits for them, and re-layouts  91.1 us (11%)
  blocking collectives  31.8 us (4%)
  between operations  22.1 us (3%)
    psum x3, waiting for transfers between devices, per_device(): lax.psum(relay_term.astype(jnp.bfloat16), 'mp').astype(jnp.float32)  206 us
    reduce_scatter x1, waiting for transfers between devices, per_device(): lax.psum_scatter(totals.astype(jnp.bfloat16), 'dp', scatter_dimension=0,...  101 us
    all_gather x1, waiting for transfers between devices, per_device(): gathered = lax.all_gather(weights, 'dp', axis=1, tiled=True)[0]  60.7 us
    dot_general x16, matrix products, project(): jnp.dot(left, right, preferred_element_type=jnp.float32)  55 us
    dynamic_update_slice x25, other arithmetic, put_row(): lax.dynamic_update_index_in_dim(buffer, jnp.where(valid, value, current),...  45.1 us
    dot_general x28, matrix products, gram(): return jnp.dot(matrix, matrix.T, preferred_element_type=jnp.float32)  42.7 us
    dynamic_slice x35, local copies, waits for them, and re-layouts, get_row(): return lax.dynamic_index_in_dim(buffer, index, 0, keepdims=False)  37.2 us
    psum x1, blocking collectives, per_device(): sq_norm = lax.psum(norm_parts, ('section', 'mp'))  31.8 us
  transfers between devices with their start and end apart: 8, of which 8 were waited for; matrix products, arithmetic and copies ran while one was open for 10% of the time, Pallas kernels for 0%

commit v1 on v0

--- a/solution.py
+++ b/solution.py
@@ -91,7 +91,9 @@
     micro_count = inputs.shape[1]
     seq_len = inputs.shape[2]
     width = inputs.shape[3]
-    gathered = lax.all_gather(weights, "dp", axis=1, tiled=True)[0]
+    gathered = jnp.concatenate(
+        lax.all_to_all(jnp.stack([weights] * lax.axis_size("dp")), "dp", 0, 0), axis=1
+    )[0]
     inner_dev = gathered.shape[2]
     own_inputs = inputs[0]
     gain_row = norm_gains[0]

time: 857 us -> 970 us (1.13)
  waiting for transfers between devices: 395 us -> 490 us
  local copies, waits for them, and re-layouts: 91.1 us -> 106 us
    all_to_all x0 -> x1, waiting for transfers between devices: none -> 156 us  [per_device(): lax.all_to_all(jnp.stack([weights] * lax.axis_size('dp')), 'dp', 0, 0)]
    all_gather x1 -> x0, waiting for transfers between devices: 60.7 us -> none  [per_device(): gathered = lax.all_gather(weights, 'dp', axis=1, tiled=True)[0]]
  transfers between devices with their start and end apart: 8 -> 8, of which waited for: 8 -> 8; matrix products, arithmetic and copies ran while one was open for 10% -> 9% of each run, Pallas kernels for 0% -> 0%
where the time goes in v1:
time: 970 us; the launch traced here: 959 us
  waiting for transfers between devices  490 us (51%)
  matrix products  198 us (20%)
  local copies, waits for them, and re-layouts  106 us (11%)
  other arithmetic  95.7 us (10%)
  blocking collectives  31.7 us (3%)
  between operations  22.1 us (2%)
  starting transfers between devices  15.5 us (2%)
    psum x3, waiting for transfers between devices, per_device(): lax.psum(relay_term.astype(jnp.bfloat16), 'mp').astype(jnp.float32)  206 us
    all_to_all x1, waiting for transfers between devices, per_device(): lax.all_to_all(jnp.stack([weights] * lax.axis_size('dp')), 'dp', 0, 0)  156 us
    reduce_scatter x1, waiting for transfers between devices, per_device(): lax.psum_scatter(totals.astype(jnp.bfloat16), 'dp', scatter_dimension=0,...  101 us
    dot_general x16, matrix products, project(): jnp.dot(left, right, preferred_element_type=jnp.float32)  50.9 us
    dynamic_update_slice x25, other arithmetic, put_row(): lax.dynamic_update_index_in_dim(buffer, jnp.where(valid, value, current),...  45.1 us
    dot_general x28, matrix products, gram(): return jnp.dot(matrix, matrix.T, preferred_element_type=jnp.float32)  42.5 us
    dynamic_slice x35, local copies, waits for them, and re-layouts, get_row(): return lax.dynamic_index_in_dim(buffer, index, 0, keepdims=False)  37.2 us
    psum x1, blocking collectives, per_device(): sq_norm = lax.psum(norm_parts, ('section', 'mp'))  31.7 us
  transfers between devices with their start and end apart: 8, of which 8 were waited for; matrix products, arithmetic and copies ran while one was open for 9% of the time, Pallas kernels for 0%

profile of v1, /device:TPU:1, one launch (start us, length us, event | category | flops | bytes accessed | tf_op | source)
XLA Modules:
  0.0 958.8 jit_solution(9097772734429967791)
XLA Ops:
  9.2 5.9 stack.41
  15.1 7.1 all-to-all-start
  49.7 155.9 %all-to-all-done = bf16[8,1,512,4,512]{4,2,3,1,0:T(8,128)(2,1)} async-done(((bf16[8,1,512,4,512]{4,2,3,1,0:T(8,128)(2,1)}), bf16[8,1,512,4,512]{4,2,3,1,0:T(8,128)(2,1)}, u32[]{:S(2)}, u32[]{:S(2)}) %all-to-all-start) | async-done | bytes 16777248 | tf_op jit(solution)/shard_map/all_to_all | solution.py:95
  205.6 8.5 copy.147
  261.1 63.2 %all-reduce.4.cloned.1.call-done = bf16[128,4096]{1,0:T(8,128)(2,1)} async-done(((bf16[128,4096]{1,0:T(8,128)(2,1)}), bf16[128,4096]{1,0:T(8,128)(2,1)}) %all-reduce.4.cloned.1.call-update) | async-done | bytes 1048592 | tf_op jit(solution)/shard_map/psum | solution.py:171
  358.5 6.0 bitcast_dynamic-update-slice_fusion.5
  412.0 4.9 conditional.4
  428.2 70.6 %all-reduce.6.cloned.1.call-done = bf16[128,4096]{1,0:T(8,128)(2,1)} async-done(((bf16[128,4096]{1,0:T(8,128)(2,1)}), bf16[128,4096]{1,0:T(8,128)(2,1)}) %all-reduce.6.cloned.1.call-update) | async-done | bytes 1048592 | tf_op jit(solution)/shard_map/psum | solution.py:171
  508.3 12.4 %collective-permute-done.1 = bf16[128,4096]{1,0:T(8,128)(2,1)S(1)} collective-permute-done((bf16[128,4096]{1,0:T(8,128)(2,1)S(1)}, bf16[128,4096]{1,0:T(8,128)(2,1)S(1)}, u32[]{:S(2)}, u32[]{:S(2)}) %collective-permute-start.1) | collective-permute-done | bytes 1048608 | tf_op jit(solution)/shard_map/ppermute | solution.py:12
  520.7 4.8 bitcast_dynamic-update-slice_fusion.4
  589.5 72.1 %all-reduce.8.cloned.1.call-done = bf16[128,4096]{1,0:T(8,128)(2,1)} async-done(((bf16[128,4096]{1,0:T(8,128)(2,1)}), bf16[128,4096]{1,0:T(8,128)(2,1)}) %all-reduce.8.cloned.1.call-update) | async-done | bytes 1048592 | tf_op jit(solution)/shard_map/psum | solution.py:171
  671.4 12.4 %collective-permute-done.2 = bf16[128,4096]{1,0:T(8,128)(2,1)S(1)} collective-permute-done((bf16[128,4096]{1,0:T(8,128)(2,1)S(1)}, bf16[128,4096]{1,0:T(8,128)(2,1)S(1)}, u32[]{:S(2)}, u32[]{:S(2)}) %collective-permute-start.2) | collective-permute-done | bytes 1048608 | tf_op jit(solution)/shard_map/ppermute | solution.py:12
  683.8 4.8 bitcast_dynamic-update-slice_fusion.3
  717.5 5.7 convolution_bitcast_fusion.1
  723.2 5.7 convolution_bitcast_fusion.5
  729.0 5.7 convolution_bitcast_fusion.2
  734.7 5.7 convolution_bitcast_fusion.6
  742.4 5.8 convolution_bitcast_fusion
  748.2 5.7 convolution_bitcast_fusion.4
  767.1 5.7 convolution_bitcast_fusion.3
  775.2 5.8 convolution_bitcast_fusion.7
  781.0 31.7 %psum.31 = f32[2]{0:T(128)S(1)} all-reduce(f32[2]{0:T(128)S(1)} %and_select_fusion.3), channel_id=1, replica_groups=mesh['section'=2,'dp'=8,'mp'=8] {'section','mp'}, use_global_device_ids=true, to_apply=%region_37.38 | all-reduce | flops 2 | bytes 16 | tf_op jit(solution)/shard_map/psum | solution.py:174
  813.4 28.8 %fusion.33 = bf16[4096,4,512]{2,0,1:T(8,128)(2,1)} fusion(f32[4096,1,512]{2,0,1:T(8,128)} %convolution_bitcast_fusion.4, f32[4096,1,512]{2,0,1:T(8,128)} %convolution_bitcast_fusion.5, f32[4096,1,512]{2,0,1:T(8,128)} %convolution_bitcast_fusion.6, f32[4096,1,512]{2,0,1:T(8,128)} %convolution_bitcast_fusion.7, f32[4096,1,512]{2,0,1:T(8,128)} %convolution_bitcast_fusion, ...), kind=kLoop, calls=%fused_computation.37 | loop fusion | flops 83886080 | bytes 83886088 | tf_op jit(solution)/shard_map/convert_element_type | solution.py:204
  842.2 100.8 %reduce-scatter.2.cloned.1.call-done = bf16[512,4,512]{2,0,1:T(8,128)(2,1)} async-done(((bf16[4096,4,512]{2,0,1:T(8,128)(2,1)}), bf16[512,4,512]{2,0,1:T(8,128)(2,1)}) %reduce-scatter.2.cloned.1.call-update) | async-done | bytes 2097168 | tf_op jit(solution)/shard_map/reduce_scatter | solution.py:203
  (315 shorter events, 315.2 us)
Async XLA Ops:
  15.1 7.2 copy-start.39
  15.1 7.2 copy-start.44
  15.1 8.6 copy-start.1
  15.1 190.5 %all-to-all-start = ((bf16[8,1,512,4,512]{4,2,3,1,0:T(8,128)(2,1)}), bf16[8,1,512,4,512]{4,2,3,1,0:T(8,128)(2,1)}, u32[]{:S(2)}, u32[]{:S(2)}) async-start(bf16[8,1,512,4,512]{4,2,3,1,0:T(8,128)(2,1)} %stack.41), calls=%async_computation | async-start | bytes 33554432 | tf_op jit(solution)/shard_map/all_to_all | solution.py:95
  22.2 302.1 %all-reduce.4.cloned.1.call-start = ((), (), s32[]{:S(2)}) async-start(), calls=%async_computation.2 | async-start | bytes 2097152 | tf_op jit(solution)/shard_map/psum | solution.py:171
  205.6 8.5 copy-start.5
  248.4 250.4 %all-reduce.6.cloned.1.call-start = ((), (), s32[]{:S(2)}) async-start(), calls=%async_computation.3 | async-start | bytes 2097152 | tf_op jit(solution)/shard_map/psum | solution.py:171
  337.9 20.6 %collective-permute-start = (bf16[128,4096]{1,0:T(8,128)(2,1)}, bf16[128,4096]{1,0:T(8,128)(2,1)}, u32[]{:S(2)}, u32[]{:S(2)}) collective-permute-start(bf16[128,4096]{1,0:T(8,128)(2,1)} %get-tuple-element.113), channel_id=1, source_target_pairs={{0,64},{64,0},{1,65},{65,1},{2,66},{66,2},{3,67},{67,3},{4,68},{68... | collective-permute-start | bytes 3145736 | tf_op jit(solution)/shard_map/ppermute | solution.py:12
  416.9 244.6 %all-reduce.8.cloned.1.call-start = ((), (), s32[]{:S(2)}) async-start(), calls=%async_computation.4 | async-start | bytes 2097152 | tf_op jit(solution)/shard_map/psum | solution.py:171
  417.7 7.4 copy-start.24
  419.3 7.3 copy-start.23
  500.3 20.3 %collective-permute-start.1 = (bf16[128,4096]{1,0:T(8,128)(2,1)S(1)}, bf16[128,4096]{1,0:T(8,128)(2,1)S(1)}, u32[]{:S(2)}, u32[]{:S(2)}) collective-permute-start(bf16[128,4096]{1,0:T(8,128)(2,1)S(1)} %fusion.67), channel_id=1, source_target_pairs={{0,64},{64,0},{1,65},{65,1},{2,66},{66,2},{3,67},{67,3},{4,68},{68... | collective-permute-start | bytes 3145736 | tf_op jit(solution)/shard_map/ppermute | solution.py:12
  505.5 15.2 %copy-start.6 = (bf16[2,128,4096]{2,1,0:T(8,128)(2,1)S(1)}, bf16[2,128,4096]{2,1,0:T(8,128)(2,1)}, u32[]{:S(2)}) copy-start(bf16[2,128,4096]{2,1,0:T(8,128)(2,1)} %param.15) | copy-start | bytes 6291460
  505.5 15.2 %copy-start.42 = (f32[128]{0:T(128)S(1)}, f32[128]{0:T(128)}, u32[]{:S(2)}) copy-start(f32[128]{0:T(128)} %add_rsqrt_fusion.1) | copy-start | bytes 1540
  505.5 15.2 %copy-start.46 = (bf16[128]{0:T(256)(128)(2,1)S(1)}, bf16[128]{0:T(256)(128)(2,1)}, u32[]{:S(2)}) copy-start(bf16[128]{0:T(256)(128)(2,1)} %compare_convert_fusion.1) | copy-start | bytes 772
  578.7 364.3 %reduce-scatter.2.cloned.1.call-start = ((), (), s32[]{:S(2)}) async-start(), calls=%async_computation.5 | async-start | bytes 18874368 | tf_op jit(solution)/shard_map/reduce_scatter | solution.py:203
  579.4 8.5 copy-start.25
  663.1 20.7 %collective-permute-start.2 = (bf16[128,4096]{1,0:T(8,128)(2,1)S(1)}, bf16[128,4096]{1,0:T(8,128)(2,1)S(1)}, u32[]{:S(2)}, u32[]{:S(2)}) collective-permute-start(bf16[128,4096]{1,0:T(8,128)(2,1)S(1)} %fusion.77), channel_id=1, source_target_pairs={{0,64},{64,0},{1,65},{65,1},{2,66},{66,2},{3,67},{67,3},{4,68},{68... | collective-permute-start | bytes 3145736 | tf_op jit(solution)/shard_map/ppermute | solution.py:12
  668.6 15.2 %copy-start.7 = (bf16[2,128,4096]{2,1,0:T(8,128)(2,1)S(1)}, bf16[2,128,4096]{2,1,0:T(8,128)(2,1)}, u32[]{:S(2)}) copy-start(bf16[2,128,4096]{2,1,0:T(8,128)(2,1)} %param.15) | copy-start | bytes 6291460
  668.6 15.2 %copy-start.41 = (f32[128]{0:T(128)S(1)}, f32[128]{0:T(128)}, u32[]{:S(2)}) copy-start(f32[128]{0:T(128)} %add_rsqrt_fusion) | copy-start | bytes 1540
  668.6 15.2 %copy-start.45 = (bf16[128]{0:T(256)(128)(2,1)S(1)}, bf16[128]{0:T(256)(128)(2,1)}, u32[]{:S(2)}) copy-start(bf16[128]{0:T(256)(128)(2,1)} %compare_convert_fusion) | copy-start | bytes 772
  702.6 9.8 %copy-start.13 = (f32[1,8,128,128]{2,3,1,0:T(8,128)S(1)}, f32[1,8,128,128]{2,3,1,0:T(8,128)}, u32[]{:S(2)}) copy-start(f32[1,8,128,128]{2,3,1,0:T(8,128)} %constant_dynamic-slice_fusion.13) | copy-start | bytes 1572868
  748.2 9.2 copy-start.22
  812.8 29.4 %copy-start.40 = (f32[2]{0:T(128)}, f32[2]{0:T(128)S(1)}, u32[]{:S(2)}) copy-start(f32[2]{0:T(128)S(1)} %add_divide_fusion) | copy-start | bytes 28
  (33 other events, 139.2 us)
Sparse Core Ops, SparseCore 0:
  248.5 75.7 all-reduce.3
  417.1 81.7 all-reduce.5
  578.9 82.6 all-reduce.7
  842.4 100.5 reduce-scatter.1
